TPU v7x, 128 devices: a whole 4x4x4 slice. The times are simulated.
128 devices in a mesh: replica: 16 (over x_lo, z, core), shard: 8 (over y, x_hi).
Axes of the slice: x: 4 (x_hi: 2, x_lo: 2; x = x_hi * 2 + x_lo), y: 4, z: 4, core: 2. Of those that a mesh axis runs over, the one named last changes fastest.
Arguments:
- weights: bfloat16 [16, 2560, 7168], P('replica', None, 'shard'), may hold values from -60 to 60, as said below
- inputs: bfloat16 [8192, 2560], P('replica'), may hold values from -0.125 to 0.125
- targets: bfloat16 [8192, 7168], P('replica', 'shard'), may hold values from -6 to 6
- factors: float32 [3, 7168, 16], P(None, 'shard'), may hold values from -6 to 6
Outputs:
- mixed: bfloat16 [16, 2560, 7168], P('replica', None, 'shard')
Inputs may be any that keep to these rules, and one draw needn't show every extreme that they name: `weights`: independent entries for every replica.
All inputs are finite; a program needn't handle non-finite values.
Results may differ from a plain program's by a relative error of at most 0.0075.
Values may be sent and summed in bfloat16 or wider, within the bound.
A program may use at most 64 MiB of HBM per device.

v0:
```python
import jax
import jax.numpy as jnp
from jax import lax
from jax.sharding import PartitionSpec as P

ROUNDS = 3
RANK = 16
DISTANCES = (1, 2, 4)
HIGH = lax.Precision.HIGHEST
F32, BF16 = (jnp.float32, jnp.bfloat16)
NT = (((1,), (1,)), ((), ()))
NN = (((1,), (0,)), ((), ()))
TN = (((0,), (0,)), ((), ()))


def mm(a, b, dims):
    return lax.dot_general(a.astype(BF16), b.astype(BF16), dims, preferred_element_type=F32)


def passed_along(value, axis, steps):
    count = lax.axis_size(axis)
    pairs = [(source, (source + steps) % count) for source in range(count)]
    return lax.ppermute(value, axis, pairs)


def orthonormal(diff):
    gram = lax.dot_general(diff, diff, NT, precision=HIGH, preferred_element_type=F32)
    lower = jnp.linalg.cholesky(gram)
    solved = lax.linalg.triangular_solve(lower, diff, left_side=True, lower=True)
    return solved.astype(BF16)


def per_device(weights, x, targets, factors):
    weight = weights[0]
    qb = factors.astype(BF16).transpose(0, 2, 1).reshape(ROUNDS * RANK, -1)
    partial = jnp.concatenate([mm(qb, weight, NT), mm(qb, targets, NT)], axis=1)
    total = lax.psum(partial, "shard")
    depth = weight.shape[0]
    shared, goal = (total[:, :depth], total[:, depth:])
    first = mm(x, weight, NN) - targets.astype(F32)
    gram_x = mm(x, x, NT)
    sums = [first]
    for _ in range(ROUNDS - 1):
        sums.append(first + sums[-1] - 0.3 * mm(gram_x, sums[-1], NN))
    grown = weight.astype(F32) - 0.3 * mm(x, sums[-1], TN)
    bases, rights = ([], [])
    for step in range(ROUNDS):
        dist = DISTANCES[step]
        shared = shared - 0.3 * mm(mm(shared, x, NT) - goal, x, NN)
        left = shared[:RANK]
        basis = orthonormal(left - passed_along(left, "replica", dist))
        shared, goal = (shared[RANK:], goal[RANK:])
        if step < ROUNDS - 1:
            inner = mm(shared, basis, NT)
            inner = inner - passed_along(inner, "replica", dist)
            shared = shared - 0.5 * mm(inner, basis, NN)
        inside = mm(basis, x, NT)
        right = mm(basis, weight, NN) - 0.3 * mm(inside, sums[step], NN)
        for old, old_right in zip(bases, rights):
            right = right - 0.5 * mm(mm(basis, old, NT), old_right, NN)
        rights.append(right - passed_along(right, "replica", dist))
        bases.append(basis)
        if step < ROUNDS - 1:
            bases = [old.astype(F32) - 0.3 * mm(mm(old, x, NT), x, NN) for old in bases]
    low_rank = mm(jnp.concatenate([b.astype(F32) for b in bases]), jnp.concatenate(rights), TN)
    return (grown - 0.5 * low_rank).astype(BF16)[None]


def solution(mesh):
    in_specs = (
        P("replica", None, "shard"),
        P("replica", None),
        P("replica", "shard"),
        P(None, "shard", None),
    )
    out_specs = P("replica", None, "shard")
    return jax.shard_map(
        per_device, mesh=mesh, in_specs=in_specs, out_specs=out_specs, check_vma=False
    )
```

profile of v0, /device:TPU:0, one launch (start us, length us, event | category | flops | bytes accessed | tf_op | source)
XLA Modules:
  0.0 217.2 jit_solution(6847564169925928657)
XLA Ops:
  7.6 3.9 %fusion.9 = f32[48,2560]{1,0:T(8,128)S(1)} fusion(bf16[48,896]{1,0:T(8,128)(2,1)S(1)} %bitcast.108, bf16[1,2560,896]{2,1,0:T(8,128)(2,1)} %param.7), kind=kOutput, calls=%fused_computation.10 | convolution fusion | flops 220200960 | bytes 5165056 | tf_op jit(solution)/shard_map/dot_general | solution.py:17
  12.8 5.2 %convert_subtract_fusion = f32[512,896]{1,0:T(8,128)S(1)} fusion(bf16[512,896]{1,0:T(8,128)(2,1)S(1)} %copy-done.8, bf16[512,2560]{1,0:T(8,128)(2,1)S(1)} %copy-done, bf16[1,2560,896]{2,1,0:T(8,128)(2,1)} %param.7), kind=kOutput, calls=%fused_computation.34 | convolution fusion | flops 2349727744 | bytes 9961472 | tf_op jit(solution)/shard_map/dot_general | solution.py:17
  20.4 2.0 multiply_subtract_fusion
  22.3 80.1 %all-reduce.2.cloned.1.call-done = f32[48,3072]{1,0:T(8,128)} async-done(((f32[48,3072]{1,0:T(8,128)}), f32[48,3072]{1,0:T(8,128)}) %all-reduce.2.cloned.1.call-update) | async-done | bytes 589840 | tf_op jit(solution)/shard_map/psum | solution.py:37
  102.4 2.6 %fusion.13 = f32[48,2560]{1,0:T(8,128)S(1)} fusion(bf16[512,2560]{1,0:T(8,128)(2,1)S(1)} %copy-done, f32[48,3072]{1,0:T(8,128)} %all-reduce.2.cloned.1.call-done), kind=kOutput, calls=%fused_computation.15 | convolution fusion | flops 252076032 | bytes 6815744 | tf_op jit(solution)/shard_map/dot_general | solution.py:17
  105.2 4.4 %subtract_convert_fusion = bf16[512,896]{1,0:T(8,128)(2,1)} fusion(f32[512,896]{1,0:T(8,128)} %copy-done.2, f32[512,896]{1,0:T(8,128)} %multiply_subtract_fusion, bf16[512,512]{1,0:T(8,128)(2,1)} %copy-done.11), kind=kOutput, calls=%fused_computation.32 | convolution fusion | flops 472055808 | bytes 5111808 | tf_op jit(solution)/shard_map/dot_general | solution.py:17
  109.6 2.4 %collective-permute-done = f32[16,2560]{1,0:T(8,128)S(1)} collective-permute-done((f32[16,2560]{1,0:T(8,128)S(1)}, f32[16,2560]{1,0:T(8,128)S(1)}, u32[]{:S(2)}, u32[]{:S(2)}) %collective-permute-start) | collective-permute-done | bytes 163872 | tf_op jit(solution)/shard_map/ppermute | solution.py:23
  117.0 3.0 %fusion.7 = f32[16,896]{1,0:T(8,128)S(1)} fusion(bf16[16,2560]{1,0:T(8,128)(2,1)S(1)} %convolution_convert_fusion.2, bf16[1,2560,896]{2,1,0:T(8,128)(2,1)} %param.7), kind=kOutput, calls=%fused_computation.8 | convolution fusion | flops 73400320 | bytes 4726784 | tf_op jit(solution)/shard_map/dot_general | solution.py:17
  122.5 1.8 fusion.19
  127.0 2.5 %fusion.14 = f32[32,2560]{1,0:T(8,128)S(1)} fusion(f32[32,2560]{1,0:T(8,128)} %fusion.15, bf16[512,2560]{1,0:T(8,128)(2,1)S(1)} %copy-done, f32[48,3072]{1,0:T(8,128)} %all-reduce.2.cloned.1.call-done), kind=kOutput, calls=%fused_computation.17 | convolution fusion | flops 168050688 | bytes 6291456 | tf_op jit(solution)/shard_map/dot_general | solution.py:17
  130.5 6.5 %collective-permute-done.2 = f32[16,2560]{1,0:T(8,128)S(1)} collective-permute-done((f32[16,2560]{1,0:T(8,128)S(1)}, f32[16,2560]{1,0:T(8,128)S(1)}, u32[]{:S(2)}, u32[]{:S(2)}) %collective-permute-start.2) | collective-permute-done | bytes 163872 | tf_op jit(solution)/shard_map/ppermute | solution.py:23
  141.8 3.0 %fusion.5 = f32[16,896]{1,0:T(8,128)S(1)} fusion(bf16[16,2560]{1,0:T(8,128)(2,1)S(1)} %convolution_convert_fusion.1, bf16[1,2560,896]{2,1,0:T(8,128)(2,1)} %param.7), kind=kOutput, calls=%fused_computation.6 | convolution fusion | flops 73400320 | bytes 4726784 | tf_op jit(solution)/shard_map/dot_general | solution.py:17
  147.8 5.4 %collective-permute-done.3 = f32[16,16]{1,0:T(8,128)S(1)} collective-permute-done((f32[16,16]{1,0:T(8,128)S(1)}, f32[16,16]{1,0:T(8,128)S(1)}, u32[]{:S(2)}, u32[]{:S(2)}) %collective-permute-start.3) | collective-permute-done | bytes 1056 | tf_op jit(solution)/shard_map/ppermute | solution.py:23
  153.3 2.0 fusion.16
  155.9 7.1 %collective-permute-done.4 = f32[16,2560]{1,0:T(8,128)S(1)} collective-permute-done((f32[16,2560]{1,0:T(8,128)S(1)}, f32[16,2560]{1,0:T(8,128)S(1)}, u32[]{:S(2)}, u32[]{:S(2)}) %collective-permute-start.4) | collective-permute-done | bytes 163872 | tf_op jit(solution)/shard_map/ppermute | solution.py:23
  164.7 2.1 cholesky.81
  171.4 3.6 %fusion.3 = f32[16,896]{1,0:T(8,128)} fusion(bf16[16,2560]{1,0:T(8,128)(2,1)S(1)} %convolution_convert_fusion, bf16[1,2560,896]{2,1,0:T(8,128)(2,1)} %param.7), kind=kOutput, calls=%fused_computation.4 | convolution fusion | flops 73400320 | bytes 4726784 | tf_op jit(solution)/shard_map/dot_general | solution.py:17
  175.0 2.5 %fusion.25 = f32[16,896]{1,0:T(8,128)} fusion(f32[16,896]{1,0:T(8,128)} %fusion.3, bf16[512,896]{1,0:T(8,128)(2,1)S(1)} %copy-done.4, bf16[16,2560]{1,0:T(8,128)(2,1)} %copy-done.5, bf16[512,2560]{1,0:T(8,128)(2,1)S(1)} %copy-done), kind=kOutput, calls=%fused_computation.44 | convolution fusion | flops 56659968 | bytes 3735552 | tf_op jit(solution)/shard_map/dot_general | solution.py:17
  177.6 1.8 fusion.24
  179.4 1.8 fusion.23
  181.3 6.1 %fusion.71 = f32[896,2560]{1,0:T(8,128)} fusion(bf16[512,896]{1,0:T(8,128)(2,1)S(1)} %copy-done.4, bf16[512,2560]{1,0:T(8,128)(2,1)S(1)} %copy-done), kind=kOutput, calls=%fused_computation.122 | convolution fusion | flops 2348810240 | bytes 12713984 | tf_op jit(solution)/shard_map/dot_general | solution.py:17
  187.4 7.3 %copy.5 = bf16[1,2560,896]{1,2,0:T(8,128)(2,1)} copy(bf16[1,2560,896]{2,1,0:T(8,128)(2,1)} %param.7) | data formatting | bytes 9175040 | tf_op args[0]
  195.6 7.5 %fusion.2 = bf16[1,2560,896]{1,2,0:T(8,128)(2,1)} fusion(f32[896,2560]{1,0:T(8,128)} %fusion.71, bf16[1,2560,896]{1,2,0:T(8,128)(2,1)} %copy.5, bf16[16,2560]{1,0:T(8,128)(2,1)S(1)} %copy-done.6, bf16[16,2560]{1,0:T(8,128)(2,1)S(1)} %copy-done.9, bf16[16,2560]{1,0:T(8,128)(2,1)S(1)} %copy-done.10, bf16[16,896]{1,0:T(8,128)(2,1)S(1)} %subtract_convert_fusion.2, ...), kind=kOutput, calls=%fused_computation.3 | convolution fusion | flops 234958848 | bytes 18681856 | tf_op jit(solution)/shard_map/dot_general | solution.py:17
  203.2 7.2 %copy.10 = bf16[1,2560,896]{2,1,0:T(8,128)(2,1)} copy(bf16[1,2560,896]{1,2,0:T(8,128)(2,1)} %fusion.2) | data formatting | bytes 9175040 | tf_op jit(solution)/shard_map/broadcast_in_dim | solution.py:66
  (93 shorter events, 31.4 us)
Async XLA Ops:
  6.5 6.3 %copy-start = (bf16[512,2560]{1,0:T(8,128)(2,1)S(1)}, bf16[512,2560]{1,0:T(8,128)(2,1)}, u32[]{:S(2)}) copy-start(bf16[512,2560]{1,0:T(8,128)(2,1)} %param.8) | copy-start | bytes 7864324
  6.5 95.9 %all-reduce.2.cloned.1.call-start = ((), (), s32[]{:S(2)}) async-start(), calls=%async_computation | async-start | bytes 1179648 | tf_op jit(solution)/shard_map/psum | solution.py:37
  7.6 3.9 %copy-start.8 = (bf16[512,896]{1,0:T(8,128)(2,1)S(1)}, bf16[512,896]{1,0:T(8,128)(2,1)}, u32[]{:S(2)}) copy-start(bf16[512,896]{1,0:T(8,128)(2,1)} %param.9) | copy-start | bytes 2752516
  18.0 1.6 copy-start.2
  19.6 0.8 copy-start.11
  105.1 6.9 %collective-permute-start = (f32[16,2560]{1,0:T(8,128)S(1)}, f32[16,2560]{1,0:T(8,128)S(1)}, u32[]{:S(2)}, u32[]{:S(2)}) collective-permute-start(f32[16,2560]{1,0:T(8,128)S(1)} %slice.42), channel_id=1, source_target_pairs={{0,8},{8,16},{16,24},{24,32},{32,40},{40,48},{48,56},{56,64},{64,7... | collective-permute-start | bytes 491528 | tf_op jit(solution)/shard_map/ppermute | solution.py:23
  120.0 1.5 copy-start.3
  120.8 5.2 %collective-permute-start.1 = (f32[32,16]{0,1:T(8,128)S(1)}, f32[32,16]{0,1:T(8,128)S(1)}, u32[]{:S(2)}, u32[]{:S(2)}) collective-permute-start(f32[32,16]{0,1:T(8,128)S(1)} %fusion.40), channel_id=1, source_target_pairs={{0,8},{8,16},{16,24},{24,32},{32,40},{40,48},{48,56},{56,64},{64,7... | collective-permute-start | bytes 6152 | tf_op jit(solution)/shard_map/ppermute | solution.py:23
  122.4 7.2 %collective-permute-start.5 = (f32[16,896]{1,0:T(8,128)}, f32[16,896]{1,0:T(8,128)}, u32[]{:S(2)}, u32[]{:S(2)}) collective-permute-start(f32[16,896]{1,0:T(8,128)} %fusion.28), channel_id=1, source_target_pairs={{0,8},{8,16},{16,24},{24,32},{32,40},{40,48},{48,56},{56,64},{64,7... | collective-permute-start | bytes 172040 | tf_op jit(solution)/shard_map/ppermute | solution.py:23
  129.5 7.5 %collective-permute-start.2 = (f32[16,2560]{1,0:T(8,128)S(1)}, f32[16,2560]{1,0:T(8,128)S(1)}, u32[]{:S(2)}, u32[]{:S(2)}) collective-permute-start(f32[16,2560]{1,0:T(8,128)S(1)} %slice.45), channel_id=1, source_target_pairs={{0,16},{8,24},{16,32},{24,40},{32,48},{40,56},{48,64},{56,72},{64,... | collective-permute-start | bytes 491528 | tf_op jit(solution)/shard_map/ppermute | solution.py:23
  130.5 16.9 %copy-start.12 = (bf16[16,896]{1,0:T(8,128)(2,1)}, bf16[16,896]{1,0:T(8,128)(2,1)S(1)}, u32[]{:S(2)}) copy-start(bf16[16,896]{1,0:T(8,128)(2,1)S(1)} %subtract_convert_fusion.4) | copy-start | bytes 86020
  144.9 2.1 copy-start.1
  147.1 6.0 %collective-permute-start.3 = (f32[16,16]{1,0:T(8,128)S(1)}, f32[16,16]{1,0:T(8,128)S(1)}, u32[]{:S(2)}, u32[]{:S(2)}) collective-permute-start(f32[16,16]{1,0:T(8,128)S(1)} %fusion.54), channel_id=1, source_target_pairs={{0,16},{8,24},{16,32},{24,40},{32,48},{40,56},{48,64},{56,72},{64,... | collective-permute-start | bytes 3080 | tf_op jit(solution)/shard_map/ppermute | solution.py:23
  147.7 7.6 %collective-permute-start.6 = (f32[16,896]{1,0:T(8,128)S(1)}, f32[16,896]{1,0:T(8,128)S(1)}, u32[]{:S(2)}, u32[]{:S(2)}) collective-permute-start(f32[16,896]{1,0:T(8,128)S(1)} %fusion.26), channel_id=1, source_target_pairs={{0,16},{8,24},{16,32},{24,40},{32,48},{40,56},{48,64},{56,72},{64,... | collective-permute-start | bytes 172040 | tf_op jit(solution)/shard_map/ppermute | solution.py:23
  155.3 7.7 %collective-permute-start.4 = (f32[16,2560]{1,0:T(8,128)S(1)}, f32[16,2560]{1,0:T(8,128)S(1)}, u32[]{:S(2)}, u32[]{:S(2)}) collective-permute-start(f32[16,2560]{1,0:T(8,128)S(1)} %fusion.16), channel_id=1, source_target_pairs={{0,32},{8,40},{16,48},{24,56},{32,64},{40,72},{48,80},{56,88},{64,... | collective-permute-start | bytes 491528 | tf_op jit(solution)/shard_map/ppermute | solution.py:23
  163.0 0.7 copy-start.7
  163.7 11.4 %copy-start.4 = (bf16[512,896]{1,0:T(8,128)(2,1)S(1)}, bf16[512,896]{1,0:T(8,128)(2,1)}, u32[]{:S(2)}) copy-start(bf16[512,896]{1,0:T(8,128)(2,1)} %subtract_convert_fusion) | copy-start | bytes 2752516
  181.3 13.5 %collective-permute-start.7 = (f32[16,896]{1,0:T(8,128)}, f32[16,896]{1,0:T(8,128)}, u32[]{:S(2)}, u32[]{:S(2)}) collective-permute-start(f32[16,896]{1,0:T(8,128)} %fusion.23), channel_id=1, source_target_pairs={{0,32},{8,40},{16,48},{24,56},{32,64},{40,72},{48,80},{56,88},{64,... | collective-permute-start | bytes 172040 | tf_op jit(solution)/shard_map/ppermute | solution.py:23
  187.4 7.4 %copy-start.15 = (f32[16,896]{1,0:T(8,128)S(1)}, f32[16,896]{1,0:T(8,128)}, u32[]{:S(2)}) copy-start(f32[16,896]{1,0:T(8,128)} %fusion.23) | copy-start | bytes 172036
  187.4 8.2 %copy-start.6 = (bf16[16,2560]{1,0:T(8,128)(2,1)S(1)}, bf16[16,2560]{1,0:T(8,128)(2,1)}, u32[]{:S(2)}) copy-start(bf16[16,2560]{1,0:T(8,128)(2,1)} %copy-done.5) | copy-start | bytes 245764
  187.4 8.2 %copy-start.9 = (bf16[16,2560]{1,0:T(8,128)(2,1)S(1)}, bf16[16,2560]{1,0:T(8,128)(2,1)}, u32[]{:S(2)}) copy-start(bf16[16,2560]{1,0:T(8,128)(2,1)} %subtract_convert_fusion.1) | copy-start | bytes 245764
  187.4 8.2 %copy-start.10 = (bf16[16,2560]{1,0:T(8,128)(2,1)S(1)}, bf16[16,2560]{1,0:T(8,128)(2,1)}, u32[]{:S(2)}) copy-start(bf16[16,2560]{1,0:T(8,128)(2,1)} %fusion.19) | copy-start | bytes 245764
  187.4 8.2 %copy-start.13 = (bf16[16,896]{1,0:T(8,128)(2,1)S(1)}, bf16[16,896]{1,0:T(8,128)(2,1)}, u32[]{:S(2)}) copy-start(bf16[16,896]{1,0:T(8,128)(2,1)} %copy-done.12) | copy-start | bytes 86020
  187.4 8.2 %copy-start.14 = (bf16[16,896]{1,0:T(8,128)(2,1)S(1)}, bf16[16,896]{1,0:T(8,128)(2,1)}, u32[]{:S(2)}) copy-start(bf16[16,896]{1,0:T(8,128)(2,1)} %subtract_convert_fusion.3) | copy-start | bytes 86020
  (1 other events, 0.6 us)
Sparse Core Ops, SparseCore 0:
  12.9 89.4 all-reduce.1
where the time goes:
time: 218 us; the launch traced here: 217 us
  waiting for transfers between devices  103 us (47%)
  matrix products  64.7 us (30%)
  other arithmetic  17.9 us (8%)
  local copies, waits for them, and re-layouts  17.1 us (8%)
  between operations  13.7 us (6%)
    psum x1, waiting for transfers between devices, per_device(): total = lax.psum(partial, 'shard')  80.1 us
    dot_general x29, matrix products, mm(): lax.dot_general(a.astype(BF16), b.astype(BF16), dims, preferred_element_t...  61.9 us
    ppermute x8, waiting for transfers between devices, passed_along(): return lax.ppermute(value, axis, pairs)  23.2 us
    unnamed x33, local copies, waits for them, and re-layouts  9.72 us
    another operation x9, other arithmetic, orthonormal(): lower = jnp.linalg.cholesky(gram)  7.34 us
    broadcast_in_dim x1, local copies, waits for them, and re-layouts, per_device(): return (grown - 0.5 * low_rank).astype(BF16)[None]  7.17 us
    another operation x6, other arithmetic, orthonormal(): lax.linalg.triangular_solve(lower, diff, left_side=True, lower=True)  5.65 us
  transfers between devices with their start and end apart: 9, of which 6 were waited for; matrix products, arithmetic and copies ran while one was open for 17% of the time, Pallas kernels for 0%

commit v1 on v0

--- a/solution.py
+++ b/solution.py
@@ -11,6 +11,12 @@
 NT = (((1,), (1,)), ((), ()))
 NN = (((1,), (0,)), ((), ()))
 TN = (((0,), (0,)), ((), ()))
+
+
+def add_all(x, mesh_axis):
+    pieces = lax.all_gather(x, mesh_axis, axis=0, tiled=False)
+    summed = pieces.sum(axis=0)
+    return summed
 
 
 def mm(a, b, dims):
@@ -34,7 +40,7 @@
     weight = weights[0]
     qb = factors.astype(BF16).transpose(0, 2, 1).reshape(ROUNDS * RANK, -1)
     partial = jnp.concatenate([mm(qb, weight, NT), mm(qb, targets, NT)], axis=1)
-    total = lax.psum(partial, "shard")
+    total = add_all(partial, "shard")
     depth = weight.shape[0]
     shared, goal = (total[:, :depth], total[:, depth:])
     first = mm(x, weight, NN) - targets.astype(F32)

time: 218 us -> 210 us (0.963)
  waiting for transfers between devices: 103 us -> 92.5 us
  other arithmetic: 17.9 us -> 21.1 us
  matrix products: 64.7 us -> 62.4 us
    psum x1 -> x0, waiting for transfers between devices: 80.1 us -> none  [per_device(): total = lax.psum(partial, 'shard')]
    all_gather x0 -> x1, waiting for transfers between devices: none -> 69.3 us  [add_all(): pieces = lax.all_gather(x, mesh_axis, axis=0, tiled=False)]
    reduce_sum x0 -> x1, other arithmetic: none -> 3.47 us  [add_all(): summed = pieces.sum(axis=0)]
    dot_general x29, matrix products: 61.9 us -> 59.6 us  [mm(): lax.dot_general(a.astype(BF16), b.astype(BF16), dims, preferred_element_t...]
    unnamed x33 -> x39, local copies, waits for them, and re-layouts: 9.72 us -> 11.1 us
where the time goes in v1:
time: 210 us; the launch traced here: 209 us
  waiting for transfers between devices  92.5 us (44%)
  matrix products  62.4 us (30%)
  other arithmetic  21.1 us (10%)
  local copies, waits for them, and re-layouts  18.5 us (9%)
  between operations  13.7 us (7%)
    all_gather x1, waiting for transfers between devices, add_all(): pieces = lax.all_gather(x, mesh_axis, axis=0, tiled=False)  69.3 us
    dot_general x29, matrix products, mm(): lax.dot_general(a.astype(BF16), b.astype(BF16), dims, preferred_element_t...  59.6 us
    ppermute x8, waiting for transfers between devices, passed_along(): return lax.ppermute(value, axis, pairs)  23.2 us
    unnamed x39, local copies, waits for them, and re-layouts  11.1 us
    another operation x9, other arithmetic, orthonormal(): lower = jnp.linalg.cholesky(gram)  7.17 us
    broadcast_in_dim x1, local copies, waits for them, and re-layouts, per_device(): return (grown - 0.5 * low_rank).astype(BF16)[None]  7.17 us
    another operation x6, other arithmetic, orthonormal(): lax.linalg.triangular_solve(lower, diff, left_side=True, lower=True)  5.47 us
  transfers between devices with their start and end apart: 9, of which 6 were waited for; matrix products, arithmetic and copies ran while one was open for 17% of the time, Pallas kernels for 0%

profile of v1, /device:TPU:0, one launch (start us, length us, event | category | flops | bytes accessed | tf_op | source)
XLA Modules:
  0.0 208.8 jit_solution(16968518541723266101)
XLA Ops:
  7.6 3.9 %fusion.9 = f32[48,2560]{1,0:T(8,128)S(1)} fusion(bf16[48,896]{1,0:T(8,128)(2,1)S(1)} %bitcast.112, bf16[1,2560,896]{2,1,0:T(8,128)(2,1)} %param.7), kind=kOutput, calls=%fused_computation.10 | convolution fusion | flops 220200960 | bytes 5165056 | tf_op jit(solution)/shard_map/dot_general | solution.py:23
  15.4 2.9 %convert_subtract_fusion = f32[512,896]{1,0:T(8,128)S(1)} fusion(bf16[512,896]{1,0:T(8,128)(2,1)S(1)} %copy-done.9, bf16[512,2560]{1,0:T(8,128)(2,1)S(1)} %copy-done, bf16[1,2560,896]{2,1,0:T(8,128)(2,1)S(1)} %bitcast.110), kind=kOutput, calls=%fused_computation.34 | convolution fusion | flops 2349727744 | bytes 9961472 | tf_op jit(solution)/shard_map/dot_general | solution.py:23
  19.5 2.0 multiply_subtract_fusion
  21.5 69.3 %all-gather.3.cloned.1.call-done = f32[384,3072]{1,0:T(8,128)} async-done(((f32[48,3072]{1,0:T(8,128)}), f32[384,3072]{1,0:T(8,128)}) %all-gather.3.cloned.1.call-update) | async-done | bytes 4718608 | tf_op jit(solution)/shard_map/all_gather | solution.py:17
  90.8 3.5 %reduce_sum.9 = f32[48,3072]{1,0:T(8,128)} reduce(f32[8,48,3072]{2,1,0:T(8,128)} %bitcast.111, f32[]{:T(128)} %constant.41.clone.1), dimensions={0}, to_apply=%region_0.0 | reduce | flops 1032192 | bytes 5308420 | tf_op jit(solution)/shard_map/reduce_sum | solution.py:18
  94.3 2.7 %fusion.13 = f32[48,2560]{1,0:T(8,128)S(1)} fusion(bf16[512,2560]{1,0:T(8,128)(2,1)S(1)} %copy-done, f32[48,3072]{1,0:T(8,128)} %reduce_sum.9), kind=kOutput, calls=%fused_computation.15 | convolution fusion | flops 252076032 | bytes 6815744 | tf_op jit(solution)/shard_map/dot_general | solution.py:23
  97.1 4.4 %subtract_convert_fusion = bf16[512,896]{1,0:T(8,128)(2,1)} fusion(f32[512,896]{1,0:T(8,128)} %copy-done.2, f32[512,896]{1,0:T(8,128)} %multiply_subtract_fusion, bf16[512,512]{1,0:T(8,128)(2,1)} %copy-done.12), kind=kOutput, calls=%fused_computation.32 | convolution fusion | flops 472055808 | bytes 5111808 | tf_op jit(solution)/shard_map/dot_general | solution.py:23
  101.5 2.4 %collective-permute-done = f32[16,2560]{1,0:T(8,128)S(1)} collective-permute-done((f32[16,2560]{1,0:T(8,128)S(1)}, f32[16,2560]{1,0:T(8,128)S(1)}, u32[]{:S(2)}, u32[]{:S(2)}) %collective-permute-start) | collective-permute-done | bytes 163872 | tf_op jit(solution)/shard_map/ppermute | solution.py:29
  108.8 3.0 %fusion.7 = f32[16,896]{1,0:T(8,128)S(1)} fusion(bf16[16,2560]{1,0:T(8,128)(2,1)S(1)} %convolution_convert_fusion.2, bf16[1,2560,896]{2,1,0:T(8,128)(2,1)} %param.7), kind=kOutput, calls=%fused_computation.8 | convolution fusion | flops 73400320 | bytes 4726784 | tf_op jit(solution)/shard_map/dot_general | solution.py:23
  118.8 2.5 %fusion.14 = f32[32,2560]{1,0:T(8,128)S(1)} fusion(f32[32,2560]{1,0:T(8,128)} %fusion.15, bf16[512,2560]{1,0:T(8,128)(2,1)S(1)} %copy-done, f32[48,3072]{1,0:T(8,128)} %reduce_sum.9), kind=kOutput, calls=%fused_computation.17 | convolution fusion | flops 168050688 | bytes 6291456 | tf_op jit(solution)/shard_map/dot_general | solution.py:23
  122.4 6.5 %collective-permute-done.2 = f32[16,2560]{1,0:T(8,128)S(1)} collective-permute-done((f32[16,2560]{1,0:T(8,128)S(1)}, f32[16,2560]{1,0:T(8,128)S(1)}, u32[]{:S(2)}, u32[]{:S(2)}) %collective-permute-start.2) | collective-permute-done | bytes 163872 | tf_op jit(solution)/shard_map/ppermute | solution.py:29
  133.8 3.0 %fusion.5 = f32[16,896]{1,0:T(8,128)S(1)} fusion(bf16[16,2560]{1,0:T(8,128)(2,1)S(1)} %convolution_convert_fusion.1, bf16[1,2560,896]{2,1,0:T(8,128)(2,1)} %param.7), kind=kOutput, calls=%fused_computation.6 | convolution fusion | flops 73400320 | bytes 4726784 | tf_op jit(solution)/shard_map/dot_general | solution.py:23
  139.6 5.4 %collective-permute-done.3 = f32[16,16]{1,0:T(8,128)S(1)} collective-permute-done((f32[16,16]{1,0:T(8,128)S(1)}, f32[16,16]{1,0:T(8,128)S(1)}, u32[]{:S(2)}, u32[]{:S(2)}) %collective-permute-start.3) | collective-permute-done | bytes 1056 | tf_op jit(solution)/shard_map/ppermute | solution.py:29
  145.1 2.0 fusion.16
  147.7 7.1 %collective-permute-done.4 = f32[16,2560]{1,0:T(8,128)S(1)} collective-permute-done((f32[16,2560]{1,0:T(8,128)S(1)}, f32[16,2560]{1,0:T(8,128)S(1)}, u32[]{:S(2)}, u32[]{:S(2)}) %collective-permute-start.4) | collective-permute-done | bytes 163872 | tf_op jit(solution)/shard_map/ppermute | solution.py:29
  156.5 2.1 %cholesky.81 = f32[16,16]{1,0:T(8,128)S(1)} custom-call(f32[16,16]{1,0:T(8,128)} %fusion.63), custom_call_target="Cholesky" | custom-call | tf_op jit(solution)/shard_map/jit(cholesky)/cholesky | solution.py:34
  163.0 3.6 %fusion.3 = f32[16,896]{1,0:T(8,128)} fusion(bf16[16,2560]{1,0:T(8,128)(2,1)S(1)} %convolution_convert_fusion, bf16[1,2560,896]{2,1,0:T(8,128)(2,1)} %param.7), kind=kOutput, calls=%fused_computation.4 | convolution fusion | flops 73400320 | bytes 4726784 | tf_op jit(solution)/shard_map/dot_general | solution.py:23
  166.7 2.5 %fusion.25 = f32[16,896]{1,0:T(8,128)} fusion(f32[16,896]{1,0:T(8,128)} %fusion.3, bf16[512,896]{1,0:T(8,128)(2,1)S(1)} %copy-done.4, bf16[16,2560]{1,0:T(8,128)(2,1)} %copy-done.5, bf16[512,2560]{1,0:T(8,128)(2,1)S(1)} %copy-done), kind=kOutput, calls=%fused_computation.44 | convolution fusion | flops 56659968 | bytes 3735552 | tf_op jit(solution)/shard_map/dot_general | solution.py:23
  169.2 1.8 fusion.24
  171.0 1.9 fusion.23
  172.9 6.1 %fusion.71 = f32[896,2560]{1,0:T(8,128)} fusion(bf16[512,896]{1,0:T(8,128)(2,1)S(1)} %copy-done.4, bf16[512,2560]{1,0:T(8,128)(2,1)S(1)} %copy-done), kind=kOutput, calls=%fused_computation.122 | convolution fusion | flops 2348810240 | bytes 12713984 | tf_op jit(solution)/shard_map/dot_general | solution.py:23
  179.0 7.3 %copy.5 = bf16[1,2560,896]{1,2,0:T(8,128)(2,1)} copy(bf16[1,2560,896]{2,1,0:T(8,128)(2,1)} %param.7) | data formatting | bytes 9175040 | tf_op args[0]
  187.3 7.5 %fusion.2 = bf16[1,2560,896]{1,2,0:T(8,128)(2,1)} fusion(f32[896,2560]{1,0:T(8,128)} %fusion.71, bf16[1,2560,896]{1,2,0:T(8,128)(2,1)} %copy.5, bf16[16,2560]{1,0:T(8,128)(2,1)S(1)} %copy-done.6, bf16[16,2560]{1,0:T(8,128)(2,1)S(1)} %copy-done.10, bf16[16,2560]{1,0:T(8,128)(2,1)S(1)} %copy-done.11, bf16[16,896]{1,0:T(8,128)(2,1)S(1)} %subtract_convert_fusion.2, ...), kind=kOutput, calls=%fused_computation.3 | convolution fusion | flops 234958848 | bytes 18681856 | tf_op jit(solution)/shard_map/dot_general | solution.py:23
  194.8 7.2 %copy.10 = bf16[1,2560,896]{2,1,0:T(8,128)(2,1)} copy(bf16[1,2560,896]{1,2,0:T(8,128)(2,1)} %fusion.2) | data formatting | bytes 9175040 | tf_op jit(solution)/shard_map/broadcast_in_dim | solution.py:72
  (101 shorter events, 34.3 us)
Async XLA Ops:
  6.5 6.3 %copy-start = (bf16[512,2560]{1,0:T(8,128)(2,1)S(1)}, bf16[512,2560]{1,0:T(8,128)(2,1)}, u32[]{:S(2)}) copy-start(bf16[512,2560]{1,0:T(8,128)(2,1)} %param.8) | copy-start | bytes 7864324
  6.5 84.3 %all-gather.3.cloned.1.call-start = ((), (), s32[]{:S(2)}) async-start(), calls=%async_computation | async-start | bytes 5308416 | tf_op jit(solution)/shard_map/all_gather | solution.py:17
  7.6 3.9 %copy-start.8 = (bf16[512,896]{1,0:T(8,128)(2,1)S(1)}, bf16[512,896]{1,0:T(8,128)(2,1)}, u32[]{:S(2)}) copy-start(bf16[512,896]{1,0:T(8,128)(2,1)} %param.9) | copy-start | bytes 2752516
  12.8 1.6 slice-start
  12.8 2.3 %slice-start.1 = ((s8[4587520]{0:T(1024)(128)(4,1)}), s8[4194304]{0:T(1024)(128)(4,1)S(1)}, s32[]{:S(2)}) async-start(s8[4587520]{0:T(1024)(128)(4,1)} %bitcast.109), calls=%async_computation.2 | async-start | bytes 8388608
  12.8 2.5 %copy-start.9 = (bf16[512,896]{1,0:T(8,128)(2,1)S(1)}, bf16[512,896]{1,0:T(8,128)(2,1)}, u32[]{:S(2)}) copy-start(bf16[512,896]{1,0:T(8,128)(2,1)} %param.9) | copy-start | bytes 2752516
  15.4 2.9 %copy-start.12 = (bf16[512,512]{1,0:T(8,128)(2,1)}, bf16[512,512]{1,0:T(8,128)(2,1)S(1)}, u32[]{:S(2)}) copy-start(bf16[512,512]{1,0:T(8,128)(2,1)S(1)} %convolution_convert_fusion.3) | copy-start | bytes 1572868
  97.0 6.9 %collective-permute-start = (f32[16,2560]{1,0:T(8,128)S(1)}, f32[16,2560]{1,0:T(8,128)S(1)}, u32[]{:S(2)}, u32[]{:S(2)}) collective-permute-start(f32[16,2560]{1,0:T(8,128)S(1)} %slice.42), channel_id=1, source_target_pairs={{0,8},{8,16},{16,24},{24,32},{32,40},{40,48},{48,56},{56,64},{64,7... | collective-permute-start | bytes 491528 | tf_op jit(solution)/shard_map/ppermute | solution.py:29
  112.6 5.2 %collective-permute-start.1 = (f32[32,16]{0,1:T(8,128)S(1)}, f32[32,16]{0,1:T(8,128)S(1)}, u32[]{:S(2)}, u32[]{:S(2)}) collective-permute-start(f32[32,16]{0,1:T(8,128)S(1)} %fusion.40), channel_id=1, source_target_pairs={{0,8},{8,16},{16,24},{24,32},{32,40},{40,48},{48,56},{56,64},{64,7... | collective-permute-start | bytes 6152 | tf_op jit(solution)/shard_map/ppermute | solution.py:29
  114.2 7.4 %collective-permute-start.5 = (f32[16,896]{1,0:T(8,128)}, f32[16,896]{1,0:T(8,128)}, u32[]{:S(2)}, u32[]{:S(2)}) collective-permute-start(f32[16,896]{1,0:T(8,128)} %fusion.28), channel_id=1, source_target_pairs={{0,8},{8,16},{16,24},{24,32},{32,40},{40,48},{48,56},{56,64},{64,7... | collective-permute-start | bytes 172040 | tf_op jit(solution)/shard_map/ppermute | solution.py:29
  121.3 7.7 %collective-permute-start.2 = (f32[16,2560]{1,0:T(8,128)S(1)}, f32[16,2560]{1,0:T(8,128)S(1)}, u32[]{:S(2)}, u32[]{:S(2)}) collective-permute-start(f32[16,2560]{1,0:T(8,128)S(1)} %slice.45), channel_id=1, source_target_pairs={{0,16},{8,24},{16,32},{24,40},{32,48},{40,56},{48,64},{56,72},{64,... | collective-permute-start | bytes 491528 | tf_op jit(solution)/shard_map/ppermute | solution.py:29
  122.4 16.7 %copy-start.13 = (bf16[16,896]{1,0:T(8,128)(2,1)}, bf16[16,896]{1,0:T(8,128)(2,1)S(1)}, u32[]{:S(2)}) copy-start(bf16[16,896]{1,0:T(8,128)(2,1)S(1)} %subtract_convert_fusion.4) | copy-start | bytes 86020
  136.8 2.1 copy-start.1
  139.1 5.8 %collective-permute-start.3 = (f32[16,16]{1,0:T(8,128)S(1)}, f32[16,16]{1,0:T(8,128)S(1)}, u32[]{:S(2)}, u32[]{:S(2)}) collective-permute-start(f32[16,16]{1,0:T(8,128)S(1)} %fusion.54), channel_id=1, source_target_pairs={{0,16},{8,24},{16,32},{24,40},{32,48},{40,56},{48,64},{56,72},{64,... | collective-permute-start | bytes 3080 | tf_op jit(solution)/shard_map/ppermute | solution.py:29
  139.5 7.6 %collective-permute-start.6 = (f32[16,896]{1,0:T(8,128)S(1)}, f32[16,896]{1,0:T(8,128)S(1)}, u32[]{:S(2)}, u32[]{:S(2)}) collective-permute-start(f32[16,896]{1,0:T(8,128)S(1)} %fusion.26), channel_id=1, source_target_pairs={{0,16},{8,24},{16,32},{24,40},{32,48},{40,56},{48,64},{56,72},{64,... | collective-permute-start | bytes 172040 | tf_op jit(solution)/shard_map/ppermute | solution.py:29
  147.0 7.7 %collective-permute-start.4 = (f32[16,2560]{1,0:T(8,128)S(1)}, f32[16,2560]{1,0:T(8,128)S(1)}, u32[]{:S(2)}, u32[]{:S(2)}) collective-permute-start(f32[16,2560]{1,0:T(8,128)S(1)} %fusion.16), channel_id=1, source_target_pairs={{0,32},{8,40},{16,48},{24,56},{32,64},{40,72},{48,80},{56,88},{64,... | collective-permute-start | bytes 491528 | tf_op jit(solution)/shard_map/ppermute | solution.py:29
  155.5 11.2 %copy-start.4 = (bf16[512,896]{1,0:T(8,128)(2,1)S(1)}, bf16[512,896]{1,0:T(8,128)(2,1)}, u32[]{:S(2)}) copy-start(bf16[512,896]{1,0:T(8,128)(2,1)} %subtract_convert_fusion) | copy-start | bytes 2752516
  172.9 13.5 %collective-permute-start.7 = (f32[16,896]{1,0:T(8,128)}, f32[16,896]{1,0:T(8,128)}, u32[]{:S(2)}, u32[]{:S(2)}) collective-permute-start(f32[16,896]{1,0:T(8,128)} %fusion.23), channel_id=1, source_target_pairs={{0,32},{8,40},{16,48},{24,56},{32,64},{40,72},{48,80},{56,88},{64,... | collective-permute-start | bytes 172040 | tf_op jit(solution)/shard_map/ppermute | solution.py:29
  179.0 7.4 %copy-start.16 = (f32[16,896]{1,0:T(8,128)S(1)}, f32[16,896]{1,0:T(8,128)}, u32[]{:S(2)}) copy-start(f32[16,896]{1,0:T(8,128)} %fusion.23) | copy-start | bytes 172036
  179.0 8.2 %copy-start.6 = (bf16[16,2560]{1,0:T(8,128)(2,1)S(1)}, bf16[16,2560]{1,0:T(8,128)(2,1)}, u32[]{:S(2)}) copy-start(bf16[16,2560]{1,0:T(8,128)(2,1)} %copy-done.5) | copy-start | bytes 245764
  179.0 8.2 %copy-start.10 = (bf16[16,2560]{1,0:T(8,128)(2,1)S(1)}, bf16[16,2560]{1,0:T(8,128)(2,1)}, u32[]{:S(2)}) copy-start(bf16[16,2560]{1,0:T(8,128)(2,1)} %subtract_convert_fusion.1) | copy-start | bytes 245764
  179.0 8.2 %copy-start.11 = (bf16[16,2560]{1,0:T(8,128)(2,1)S(1)}, bf16[16,2560]{1,0:T(8,128)(2,1)}, u32[]{:S(2)}) copy-start(bf16[16,2560]{1,0:T(8,128)(2,1)} %fusion.19) | copy-start | bytes 245764
  179.0 8.2 %copy-start.14 = (bf16[16,896]{1,0:T(8,128)(2,1)S(1)}, bf16[16,896]{1,0:T(8,128)(2,1)}, u32[]{:S(2)}) copy-start(bf16[16,896]{1,0:T(8,128)(2,1)} %copy-done.13) | copy-start | bytes 86020
  179.0 8.2 %copy-start.15 = (bf16[16,896]{1,0:T(8,128)(2,1)S(1)}, bf16[16,896]{1,0:T(8,128)(2,1)}, u32[]{:S(2)}) copy-start(bf16[16,896]{1,0:T(8,128)(2,1)} %subtract_convert_fusion.3) | copy-start | bytes 86020
  (4 other events, 4.1 us)
Sparse Core Ops, SparseCore 0:
  12.9 77.8 all-gather.2
